TPU v7x, 32 devices: a whole 2x2x4 slice. The times are simulated.
32 devices in a mesh: groups: 2 (over x), expert: 16 (over z, y, core).
Axes of the slice: x: 2, y: 2, z: 4, core: 2. Of those that a mesh axis runs over, the one named last changes fastest.
Arguments:
- tokens: bfloat16 [256, 7168], P(('groups', 'expert')), parts along dimension 0, may hold values from -6 to 6
- expert_ids: int32 [256, 2], P(('groups', 'expert')), parts along dimension 0, may hold values from 0 to 3, as said below
- gate_scores: float32 [256, 2], P(('groups', 'expert')), parts along dimension 0, may hold values from 0.2 to 1
- w_gate_up: bfloat16 [16, 7168, 512], P('expert'), may hold values from -0.0625 to 0.0625
- w_down: bfloat16 [16, 256, 7168], P('expert'), may hold values from -0.1875 to 0.1875
Outputs:
- moe_out: bfloat16 [256, 7168], P(('groups', 'expert')), parts along dimension 0
There are 2 independent parts, one for each index of `groups`. A program takes and returns all parts, laid end to end along the dimension named above; an argument that names none is the same for every part. Nothing has to cross between parts.
Inputs may be any that keep to these rules, and one draw needn't show every extreme that they name: `expert_ids`: each row names 2 different experts. In each aligned block of 8 rows (the rows of one device) no expert is named by more than 8 rows, and one expert is named by exactly 8 rows in every block.
All inputs are finite; a program needn't handle non-finite values.
Results may differ from a plain program's by a relative error of at most 0.0058.
Values may be sent and summed in bfloat16 or wider, within the bound.
A program may use at most 128 MiB of HBM per device.

v0:
```python
import jax
import jax.numpy as jnp
from jax import lax
from jax.sharding import PartitionSpec as P

SPLIT = 4


route_scale = 2.5


def expert_block(block_tokens, gate_up_part, down_part):
    hidden_width = down_part.shape[0]
    gate_up = jnp.dot(block_tokens, gate_up_part, preferred_element_type=jnp.float32)
    hidden = (jax.nn.silu(gate_up[:, :hidden_width]) * gate_up[:, hidden_width:]).astype(
        jnp.bfloat16
    )
    return jnp.dot(hidden, down_part, preferred_element_type=jnp.float32).astype(jnp.bfloat16)


def rank_within(values_in, class_count):
    one_hot = (values_in[:, None] == jnp.arange(class_count, dtype=jnp.int32)[None, :]).astype(
        jnp.int32
    )
    earlier = jnp.cumsum(one_hot, axis=0) - one_hot
    return jnp.sum(earlier * one_hot, axis=1)


def serve(flat_rows, flat_labels, label_value, gate_up_part, down_part, results):
    finished = expert_block(flat_rows, gate_up_part, down_part)
    served_rows = jnp.where((flat_labels == label_value)[:, None], finished, results)
    return served_rows


def body(tokens, expert_ids, gate_scores, w_gate_up, w_down):
    dev_count = lax.axis_size("expert")
    rows_dev = expert_ids.shape[0]
    route_count = expert_ids.shape[1]
    model_width = tokens.shape[1]
    expert_count = dev_count // SPLIT
    slot_count = 2 * rows_dev * route_count // expert_count
    group_slots = expert_count * slot_count
    slot_total = dev_count * slot_count
    weights = route_scale * gate_scores / jnp.sum(gate_scores, axis=1, keepdims=True)
    flat_ids = expert_ids.reshape(-1)
    home_gate_up = w_gate_up[0]
    home_down = w_down[0]
    route_label = jnp.zeros_like(flat_ids)
    served = ((0, home_gate_up, home_down),)
    rank = rank_within(flat_ids, expert_count)
    target = flat_ids * slot_count + rank
    route_rows = jnp.arange(rows_dev * route_count, dtype=jnp.int32) // route_count
    source_of = jnp.full((group_slots,), rows_dev, jnp.int32).at[target].set(route_rows)
    label_of = jnp.full((group_slots,), -1, jnp.int32).at[target].set(route_label)
    outgoing = jnp.take(tokens, source_of, axis=0, mode="fill", fill_value=0)
    outgoing = jnp.broadcast_to(
        outgoing.reshape(expert_count, 1, slot_count, model_width),
        (expert_count, SPLIT, slot_count, model_width),
    ).reshape(dev_count, slot_count, model_width)
    label_out = jnp.broadcast_to(
        label_of.reshape(expert_count, 1, slot_count), (expert_count, SPLIT, slot_count)
    ).reshape(dev_count, slot_count)
    arrived, labels = (
        lax.all_to_all(outgoing, "expert", split_axis=0, concat_axis=0, tiled=True),
        lax.all_to_all(label_out, "expert", split_axis=0, concat_axis=0, tiled=True),
    )
    flat_rows = arrived.reshape(slot_total, model_width)
    flat_labels = labels.reshape(slot_total)
    results = jnp.zeros((slot_total, model_width), jnp.bfloat16)
    label_value, gate_up_part, down_part = served[0]
    results = serve(flat_rows, flat_labels, label_value, gate_up_part, down_part, results)
    returned = lax.all_to_all(
        results.reshape(dev_count, slot_count, model_width),
        "expert",
        split_axis=0,
        concat_axis=0,
        tiled=True,
    )
    grouped = returned.reshape(expert_count, SPLIT, slot_count, model_width)
    picked = grouped[flat_ids, :, rank]
    expert_out = jnp.sum(picked.astype(jnp.float32), axis=1).reshape(
        rows_dev, route_count, model_width
    )
    combined = jnp.sum(weights[:, :, None] * expert_out, axis=1)
    return combined.astype(jnp.bfloat16)


def solution(mesh):
    in_specs = (
        P(("groups", "expert"), None),
        P(("groups", "expert"), None),
        P(("groups", "expert"), None),
        P("expert", None, None),
        P("expert", None, None),
    )
    out_specs = P(("groups", "expert"), None)
    return jax.shard_map(body, mesh=mesh, in_specs=in_specs, out_specs=out_specs, check_vma=False)
```

profile of v0, /device:TPU:13, one launch (start us, length us, event | category | flops | bytes accessed | tf_op | source)
XLA Modules:
  0.0 123.6 jit_solution(11272302360567906375)
XLA Ops:
  0.0 0.0 copy-start
  0.0 0.8 copy.26
  0.8 0.1 eq.28
  0.9 0.1 reshape.121
  1.0 0.1 fusion.9
  1.1 0.2 select_reduce_fusion
  1.3 0.6 scatter_custom_fusion
  1.9 0.1 broadcast_in_dim.52
  2.0 0.6 broadcast_in_dim.53
  2.6 6.5 %all-to-all-start = ((s32[16,1,8]{2,1,0:T(1,128)}), s32[16,1,8]{2,1,0:T(1,128)S(1)}, u32[]{:S(2)}, u32[]{:S(2)}) async-start(s32[16,1,8]{2,1,0:T(1,128)} %bitcast.3), calls=%async_computation | async-start | bytes 16384 | tf_op jit(solution)/shard_map/all_to_all | solution.py:65
  9.1 0.6 scatter_custom_fusion.1
  9.8 0.1 broadcast_in_dim.56
  9.9 0.0 copy-done
  9.9 0.8 gather_fusion
  10.7 0.1 bitcast_select_fusion
  10.8 2.1 %all-to-all-done = s32[16,1,8]{2,1,0:T(1,128)S(1)} async-done(((s32[16,1,8]{2,1,0:T(1,128)}), s32[16,1,8]{2,1,0:T(1,128)S(1)}, u32[]{:S(2)}, u32[]{:S(2)}) %all-to-all-start) | async-done | bytes 544 | tf_op jit(solution)/shard_map/all_to_all | solution.py:65
  12.9 1.4 %broadcast_in_dim.60 = bf16[4,4,8,7168]{3,2,1,0:T(8,128)(2,1)} broadcast(bf16[4,8,7168]{2,1,0:T(8,128)(2,1)S(1)} %bitcast_select_fusion), dimensions={0,2,3} | broadcast | bytes 2293760 | tf_op jit(solution)/shard_map/broadcast_in_dim | solution.py:56
  14.3 6.2 %all-to-all-start.1 = ((bf16[16,8,7168]{2,1,0:T(8,128)(2,1)}), bf16[16,8,7168]{2,1,0:T(8,128)(2,1)S(1)}, u32[]{:S(2)}, u32[]{:S(2)}) async-start(bf16[16,8,7168]{2,1,0:T(8,128)(2,1)} %bitcast.30), calls=%async_computation.1 | async-start | bytes 3670016 | tf_op jit(solution)/shard_map/all_to_all | solution.py:64
  20.6 0.1 eq.34
  20.7 41.7 %all-to-all-done.1 = bf16[16,8,7168]{2,1,0:T(8,128)(2,1)S(1)} async-done(((bf16[16,8,7168]{2,1,0:T(8,128)(2,1)}), bf16[16,8,7168]{2,1,0:T(8,128)(2,1)S(1)}, u32[]{:S(2)}, u32[]{:S(2)}) %all-to-all-start.1) | async-done | bytes 1835040 | tf_op jit(solution)/shard_map/all_to_all | solution.py:64
  62.4 0.0 copy-start.1
  62.4 4.3 %fusion.2 = f32[128,512]{1,0:T(8,128)S(1)} fusion(bf16[1,7168,512]{2,1,0:T(8,128)(2,1)} %param.8, bf16[16,8,7168]{2,1,0:T(8,128)(2,1)S(1)} %all-to-all-done.1), kind=kOutput, calls=%fused_computation.7 | convolution fusion | flops 939524096 | bytes 9437184 | tf_op jit(solution)/shard_map/dot_general | solution.py:14
  66.7 0.0 copy-done.1
  66.7 1.9 %fusion.1 = bf16[16,8,7168]{2,1,0:T(8,128)(2,1)} fusion(bf16[1,256,7168]{2,1,0:T(8,128)(2,1)S(1)} %copy-done.1, pred[128]{0:T(512)(128)(4,1)S(1)} %eq.34, f32[128,512]{1,0:T(8,128)S(1)} %fusion.2), kind=kOutput, calls=%fused_computation.6 | convolution fusion | flops 471793664 | bytes 5767296 | tf_op jit(solution)/shard_map/dot_general | solution.py:18
  68.7 0.0 copy-start.2
  68.7 4.9 %all-to-all-start.2 = ((bf16[16,8,7168]{2,1,0:T(8,128)(2,1)}), bf16[16,8,7168]{2,1,0:T(8,128)(2,1)S(1)}, u32[]{:S(2)}, u32[]{:S(2)}) async-start(bf16[16,8,7168]{2,1,0:T(8,128)(2,1)} %fusion.1), calls=%async_computation.2 | async-start | bytes 3670016 | tf_op jit(solution)/shard_map/all_to_all | solution.py:72
  73.6 0.0 copy-done.2
  73.6 0.1 copy.25
  73.7 41.7 %all-to-all-done.2 = bf16[16,8,7168]{2,1,0:T(8,128)(2,1)S(1)} async-done(((bf16[16,8,7168]{2,1,0:T(8,128)(2,1)}), bf16[16,8,7168]{2,1,0:T(8,128)(2,1)S(1)}, u32[]{:S(2)}, u32[]{:S(2)}) %all-to-all-start.2) | async-done | bytes 1835040 | tf_op jit(solution)/shard_map/all_to_all | solution.py:72
  115.4 2.7 %copy.29 = bf16[4,4,8,7168]{3,1,2,0:T(4,128)(2,1)} copy(bf16[4,4,8,7168]{3,2,1,0:T(8,128)(2,1)S(1)} %bitcast.29) | data formatting | bytes 3670016 | tf_op jit(solution)/shard_map/reshape | solution.py:79
  118.0 2.8 %gather_fusion.1 = bf16[16,4,7168]{2,1,0:T(4,128)(2,1)S(1)} fusion(bf16[4,4,8,7168]{3,1,2,0:T(4,128)(2,1)} %copy.29, s32[16]{0:T(128)S(1)} %get-tuple-element.5), kind=kCustom, calls=%fused_computation.1 | custom fusion | bytes 1835136 | tf_op jit(solution)/shard_map/gather | solution.py:80
  120.9 1.2 convert_reduce_fusion
  122.1 0.3 reshape.126
  122.3 1.3 %multiply_reduce_fusion = bf16[8,7168]{1,0:T(8,128)(2,1)} fusion(f32[8,2,7168]{2,1,0:T(2,128)S(1)} %reshape.126, f32[8,2]{1,0:T(8,128)S(1)} %copy.25), kind=kLoop, calls=%fused_computation.13 | loop fusion | flops 172032 | bytes 573504 | tf_op jit(solution)/shard_map/reduce_sum | solution.py:84
  (10 shorter events, 0.1 us)
Async XLA Ops:
  0.0 9.9 %copy-start = (bf16[8,7168]{1,0:T(8,128)(2,1)S(1)}, bf16[8,7168]{1,0:T(8,128)(2,1)}, u32[]{:S(2)}) copy-start(bf16[8,7168]{1,0:T(8,128)(2,1)} %param.5) | copy-start | bytes 344068
  2.6 10.3 %all-to-all-start = ((s32[16,1,8]{2,1,0:T(1,128)}), s32[16,1,8]{2,1,0:T(1,128)S(1)}, u32[]{:S(2)}, u32[]{:S(2)}) async-start(s32[16,1,8]{2,1,0:T(1,128)} %bitcast.3), calls=%async_computation | async-start | bytes 16384 | tf_op jit(solution)/shard_map/all_to_all | solution.py:65
  14.3 48.0 %all-to-all-start.1 = ((bf16[16,8,7168]{2,1,0:T(8,128)(2,1)}), bf16[16,8,7168]{2,1,0:T(8,128)(2,1)S(1)}, u32[]{:S(2)}, u32[]{:S(2)}) async-start(bf16[16,8,7168]{2,1,0:T(8,128)(2,1)} %bitcast.30), calls=%async_computation.1 | async-start | bytes 3670016 | tf_op jit(solution)/shard_map/all_to_all | solution.py:64
  62.4 4.4 %copy-start.1 = (bf16[1,256,7168]{2,1,0:T(8,128)(2,1)S(1)}, bf16[1,256,7168]{2,1,0:T(8,128)(2,1)}, u32[]{:S(2)}) copy-start(bf16[1,256,7168]{2,1,0:T(8,128)(2,1)} %param.9) | copy-start | bytes 11010052
  68.7 4.9 %copy-start.2 = (f32[8,2]{0,1:T(2,128)S(1)}, f32[8,2]{0,1:T(2,128)}, u32[]{:S(2)}) copy-start(f32[8,2]{0,1:T(2,128)} %param.7) | copy-start | bytes 196
  68.7 46.7 %all-to-all-start.2 = ((bf16[16,8,7168]{2,1,0:T(8,128)(2,1)}), bf16[16,8,7168]{2,1,0:T(8,128)(2,1)S(1)}, u32[]{:S(2)}, u32[]{:S(2)}) async-start(bf16[16,8,7168]{2,1,0:T(8,128)(2,1)} %fusion.1), calls=%async_computation.2 | async-start | bytes 3670016 | tf_op jit(solution)/shard_map/all_to_all | solution.py:72
where the time goes:
time: 124 us
  waiting for transfers between devices  85.4 us (69%)
  starting transfers between devices  17.6 us (14%)
  local copies, waits for them, and re-layouts  11.2 us (9%)
  matrix products  6.28 us (5%)
  other arithmetic  2.96 us (2%)
    all_to_all x1, waiting for transfers between devices, body(): lax.all_to_all(outgoing, 'expert', split_axis=0, concat_axis=0, tiled=True)  41.7 us
    all_to_all x1, waiting for transfers between devices, body(): lax.all_to_all(results.reshape(dev_count, slot_count, model_width), 'expe...  41.7 us
    all_to_all x1, starting transfers between devices, body(): lax.all_to_all(label_out, 'expert', split_axis=0, concat_axis=0, tiled=True)  6.52 us
    all_to_all x1, starting transfers between devices, body(): lax.all_to_all(outgoing, 'expert', split_axis=0, concat_axis=0, tiled=True)  6.21 us
    all_to_all x1, starting transfers between devices, body(): lax.all_to_all(results.reshape(dev_count, slot_count, model_width), 'expe...  4.9 us
    dot_general x1, matrix products, expert_block(): jnp.dot(block_tokens, gate_up_part, preferred_element_type=jnp.float32)  4.35 us
    gather x1, local copies, waits for them, and re-layouts, body(): picked = grouped[flat_ids, :, rank]  2.83 us
    reshape x1, local copies, waits for them, and re-layouts, body(): grouped = returned.reshape(expert_count, SPLIT, slot_count, model_width)  2.67 us
  transfers between devices with their start and end apart: 3, of which 3 were waited for; matrix products, arithmetic and copies ran while one was open for 2% of the time, Pallas kernels for 0%

commit v1 on v0

v1 whole, which is shorter than its diff:
```python
import functools

import jax
import jax.numpy as jnp
from jax import lax
from jax.experimental import pallas as pl
from jax.experimental.pallas import tpu as pltpu
from jax.sharding import PartitionSpec as P

SPLIT = 4
ROUTE_SCALE = 2.5
TILE = 256


def ring_chip(position, chips, folded):
    if not folded:
        return position
    length = chips // 2
    side = position // length
    along = position % length
    return (along + side * (length - 1 - 2 * along)) * 2 + side


def ring_position(chip, chips, folded):
    if not folded:
        return chip
    length = chips // 2
    along = chip // 2
    side = chip % 2
    return along + side * (chips - 1 - 2 * along)


def kernel(n, chunks, folded, tokens_ref, route_ref, wg_hbm, wd_hbm, out_ref,
           x, routes, wg, wd, gate_up, hidden, column, own, to_sib, from_sib, outgoing, incoming,
           wg_sem, wd_sem, ag_send, ag_recv, sib_send, sib_recv,
           rt_send, rt_recv, rts_send, rts_recv, xs_send, xs_recv, rs_send, rs_recv):
    chips = n // 2
    half = chips // 2
    rows, width = tokens_ref.shape
    step = width // chunks
    ring_rows = chips * rows
    hid = wd.shape[0]

    me = lax.axis_index("expert")
    core = me % 2
    pos = ring_position(me // 2, chips, folded)
    right = ring_chip((pos + 1) % chips, chips, folded) * 2 + core
    left = ring_chip((pos + chips - 1) % chips, chips, folded) * 2 + core
    sib = me + 1 - 2 * core
    peer = (right, left)

    wg_copies = [
        pltpu.make_async_copy(wg_hbm.at[0, pl.ds(c * step, step), :],
                              wg.at[pl.ds(c * step, step), :], wg_sem.at[c])
        for c in range(chunks)
    ]
    wd_copies = [
        pltpu.make_async_copy(wd_hbm.at[0, :, pl.ds(c * step, step)],
                              wd.at[:, pl.ds(c * step, step)], wd_sem.at[c])
        for c in range(chunks)
    ]

    barrier = pltpu.get_barrier_semaphore()
    for other in (left, right, sib):
        pl.semaphore_signal(barrier, inc=1, device_id={"expert": other},
                            device_id_type=pl.DeviceIdType.MESH)
    for copy in wg_copies:
        copy.start()
    for copy in wd_copies:
        copy.start()
    pl.semaphore_wait(barrier, 3)

    def remote(src, dst, send, recv, device):
        return pltpu.make_async_remote_copy(
            src_ref=src, dst_ref=dst, send_sem=send, recv_sem=recv,
            device_id={"expert": device}, device_id_type=pl.DeviceIdType.MESH)

    def reach(way, c):
        return half if (c < chunks // 2) == (way == 0) else half - 1

    def slot_of(way, d):
        return d if way == 0 else (chips - d) % chips

    def block(ref, slot, c):
        return ref.at[pl.ds(slot * rows, rows), pl.ds(c * step, step)]

    def route_block(slot):
        return routes.at[pl.ds(slot * rows, rows), :]

    sends = []

    def ag_copy(way, d, c):
        src = (tokens_ref.at[:, pl.ds(c * step, step)] if d == 1
               else block(x, slot_of(way, d - 1), c))
        return remote(src, block(x, slot_of(way, d), c),
                      ag_send.at[way, d - 1, c], ag_recv.at[way, d - 1, c], peer[way])

    def sib_copy(slot, c):
        src = (tokens_ref.at[:, pl.ds(c * step, step)] if slot == 0 else block(x, slot, c))
        return remote(src, block(x, chips + slot, c),
                      sib_send.at[slot, c], sib_recv.at[slot, c], sib)

    def rt_copy(way, d):
        src = route_ref if d == 1 else route_block(slot_of(way, d - 1))
        return remote(src, route_block(slot_of(way, d)),
                      rt_send.at[way, d - 1], rt_recv.at[way, d - 1], peer[way])

    def rts_copy(slot):
        src = route_ref if slot == 0 else route_block(slot)
        return remote(src, route_block(chips + slot), rts_send.at[slot], rts_recv.at[slot], sib)

    def go(copy):
        copy.start()
        sends.append(copy)

    for c in range(chunks):
        for way in range(2):
            go(ag_copy(way, 1, c))
        if c == 0:
            for way in range(2):
                go(rt_copy(way, 1))
    for c in range(chunks):
        go(sib_copy(0, c))
    go(rts_copy(0))
    x[pl.ds(0, rows), :] = tokens_ref[...]
    routes[pl.ds(0, rows), :] = route_ref[...]

    order = [c for pair in zip(range(chunks // 2), range(chunks // 2, chunks)) for c in pair]
    for d in range(1, half + 1):
        for c in order:
            for way in range(2):
                if d > reach(way, c):
                    continue
                ag_copy(way, d, c).wait_recv()
                if d + 1 <= reach(way, c):
                    go(ag_copy(way, d + 1, c))
                go(sib_copy(slot_of(way, d), c))
        for way in range(2):
            far = half if way == 0 else half - 1
            if d <= far:
                rt_copy(way, d).wait_recv()
                if d + 1 <= far:
                    go(rt_copy(way, d + 1))
                go(rts_copy(slot_of(way, d)))

    for index, c in enumerate(order):
        for slot in range(chips):
            sib_copy(slot, c).wait_recv()
        wg_copies[c].wait()
        part = jnp.dot(x[:, pl.ds(c * step, step)], wg[pl.ds(c * step, step), :],
                       preferred_element_type=jnp.float32)
        if index == 0:
            gate_up[...] = part
        else:
            gate_up[...] += part
    for slot in range(chips):
        rts_copy(slot).wait_recv()
    gate = gate_up[:, :hid]
    hidden[...] = (gate / (1.0 + jnp.exp(-gate)) * gate_up[:, hid:]).astype(jnp.bfloat16)
    lane = lax.broadcasted_iota(jnp.int32, routes.shape, 1)
    column[...] = jnp.sum(jnp.where(lane == me // SPLIT, routes[...], 0.0), axis=1, keepdims=True)

    def down(c):
        wd_copies[c].wait()

        def tile(t, carry):
            cols = pl.ds(pl.multiple_of(c * step + t * TILE, TILE), TILE)
            part = column[...] * jnp.dot(hidden[...], wd[:, cols],
                                         preferred_element_type=jnp.float32)
            own[:, cols] = part[:ring_rows]
            to_sib[:, cols] = part[ring_rows:].astype(jnp.bfloat16)
            return carry

        lax.fori_loop(0, step // TILE, tile, 0)

    def exchange(c):
        cols = pl.ds(c * step, step)
        return remote(to_sib.at[:, cols], from_sib.at[:, cols], xs_send.at[c], xs_recv.at[c], sib)

    def rs_copy(way, k, c):
        slot = slot_of(1 - way, k)
        return remote(block(outgoing, slot, c), block(incoming, way * half + k - 1, c),
                      rs_send.at[way, k - 1, c], rs_recv.at[way, k - 1, c], peer[way])

    def piece(slot, c):
        return (pl.ds(slot * rows, rows), pl.ds(c * step, step))

    def heads(c):
        cols = pl.ds(c * step, step)
        exchange(c).wait_recv()
        for way in range(2):
            k = reach(way, c)
            at = piece(slot_of(1 - way, k), c)
            outgoing[at] = (own[at] + from_sib[at].astype(jnp.float32)).astype(jnp.bfloat16)
            go(rs_copy(way, k, c))

    for index, c in enumerate(order):
        down(c)
        go(exchange(c))
        if index:
            heads(order[index - 1])
    heads(order[-1])

    for r in range(1, half + 1):
        for c in order:
            for way in range(2):
                k = reach(way, c) - r
                if k < 1:
                    continue
                rs_copy(way, k + 1, c).wait_recv()
                at = piece(slot_of(1 - way, k), c)
                arrived = piece(way * half + k, c)
                outgoing[at] = (own[at] + from_sib[at].astype(jnp.float32)
                                + incoming[arrived].astype(jnp.float32)).astype(jnp.bfloat16)
                go(rs_copy(way, k, c))
    for c in order:
        at = piece(0, c)
        total = own[at] + from_sib[at].astype(jnp.float32)
        for way in range(2):
            rs_copy(way, 1, c).wait_recv()
            total = total + incoming[piece(way * half, c)].astype(jnp.float32)
        out_ref[:, pl.ds(c * step, step)] = total.astype(jnp.bfloat16)
    for copy in sends:
        copy.wait_send()


def body(n, tokens, expert_ids, gate_scores, w_gate_up, w_down):
    rows, width = tokens.shape
    hid = w_down.shape[1]
    chips = n // 2
    half = chips // 2
    folded = chips == 8
    chunks = 4 if n <= 16 else 2
    weights = ROUTE_SCALE * gate_scores / jnp.sum(gate_scores, axis=1, keepdims=True)
    named = expert_ids[:, :, None] == jnp.arange(128, dtype=jnp.int32)[None, None, :]
    routed = jnp.sum(jnp.where(named, weights[:, :, None], 0.0), axis=1)
    vmem, dma = pltpu.VMEM, pltpu.SemaphoreType.DMA
    bf16, f32 = jnp.bfloat16, jnp.float32
    return pl.pallas_call(
        functools.partial(kernel, n, chunks, folded),
        out_shape=jax.ShapeDtypeStruct((rows, width), bf16),
        in_specs=[
            pl.BlockSpec(memory_space=pltpu.VMEM),
            pl.BlockSpec(memory_space=pltpu.VMEM),
            pl.BlockSpec(memory_space=pl.ANY),
            pl.BlockSpec(memory_space=pl.ANY),
        ],
        out_specs=pl.BlockSpec(memory_space=pltpu.VMEM),
        scratch_shapes=[
            vmem((n * rows, width), bf16),
            vmem((n * rows, 128), f32),
            vmem((width, 2 * hid), bf16),
            vmem((hid, width), bf16),
            vmem((n * rows, 2 * hid), f32),
            vmem((n * rows, hid), bf16),
            vmem((n * rows, 1), f32),
            vmem((chips * rows, width), f32),
            vmem((chips * rows, width), bf16),
            vmem((chips * rows, width), bf16),
            vmem((chips * rows, width), bf16),
            vmem((2 * half * rows, width), bf16),
            dma((chunks,)), dma((chunks,)),
            dma((2, half, chunks)), dma((2, half, chunks)),
            dma((chips, chunks)), dma((chips, chunks)),
            dma((2, half)), dma((2, half)),
            dma((chips,)), dma((chips,)),
            dma((chunks,)), dma((chunks,)),
            dma((2, half, chunks)), dma((2, half, chunks)),
        ],
        compiler_params=pltpu.CompilerParams(collective_id=0, has_side_effects=True),
        name="routed_experts",
    )(tokens, routed, w_gate_up, w_down)


def solution(mesh):
    in_specs = (
        P(("groups", "expert"), None),
        P(("groups", "expert"), None),
        P(("groups", "expert"), None),
        P("expert", None, None),
        P("expert", None, None),
    )
    out_specs = P(("groups", "expert"), None)
    return jax.shard_map(
        functools.partial(body, mesh.shape["expert"]),
        mesh=mesh, in_specs=in_specs, out_specs=out_specs, check_vma=False)
```

time: 124 us -> 46.5 us (0.38)
  the two profiles are of different devices: /device:TPU:13 before, /device:TPU:0 now
where the time goes in v1:
time: 46.5 us; the launch traced here: 46.3 us
  Pallas kernels  42 us (90%)
  other arithmetic  2.73 us (6%)
  local copies, waits for them, and re-layouts  1.55 us (3%)
    pallas_call x1, Pallas kernels, body(): pl.pallas_call(functools.partial(kernel, n, chunks, folded), out_shape=ja...  42 us
    unnamed x1, local copies, waits for them, and re-layouts  1.55 us
    reduce_sum x1, other arithmetic, body(): routed = jnp.sum(jnp.where(named, weights[:, :, None], 0.0), axis=1)  1.35 us

profile of v1, /device:TPU:0, one launch (start us, length us, event | category | flops | bytes accessed | tf_op | source)
XLA Modules:
  0.0 46.3 jit_solution(10857328813107887288)
XLA Ops:
  0.0 0.7 %reduce_sum.18 = f32[8]{0:T(128)S(1)} reduce(f32[8,2]{0,1:T(2,128)} %param.7, f32[]{:T(128)} %constant.1.clone.1), dimensions={1}, to_apply=%region_0.0 | reduce | flops 8 | bytes 100 | tf_op jit(solution)/shard_map/reduce_sum | solution.py:234
  0.7 0.7 %multiply_divide_fusion = f32[8,2]{0,1:T(2,128)S(1)} fusion(f32[8,2]{0,1:T(2,128)} %param.7, f32[8]{0:T(128)S(1)} %reduce_sum.18), kind=kLoop, calls=%fused_computation.2 | loop fusion | flops 32 | bytes 160 | tf_op jit(solution)/shard_map/div | solution.py:234
  1.4 1.3 %select_reduce_fusion.route_ref = f32[8,128]{1,0:T(8,128)} fusion(f32[8,2]{0,1:T(2,128)S(1)} %multiply_divide_fusion, s32[8,2]{0,1:T(2,128)} %param.6), kind=kLoop, calls=%fused_computation | loop fusion | flops 5120 | bytes 4224 | tf_op jit(solution)/shard_map/reduce_sum | solution.py:236
  2.7 42.0 %routed_experts.1 = bf16[8,7168]{1,0:T(8,128)(2,1)} custom-call(bf16[8,7168]{1,0:T(8,128)(2,1)} %tokens_ref.1, f32[8,128]{1,0:T(8,128)} %select_reduce_fusion.route_ref, bf16[1,7168,512]{2,1,0:T(8,128)(2,1)} %wg_hbm.1, bf16[1,256,7168]{2,1,0:T(8,128)(2,1)} %wd_hbm.1), custom_call_target="tpu_custom_call" | custom-call | tf_op jit(solution)/shard_map/routed_experts/pallas_call | solution.py:239
  44.7 1.6 %copy.9 = bf16[8,7168]{1,0:T(8,128)(2,1)} copy(bf16[8,7168]{1,0:T(8,128)(2,1)} %routed_experts.1) | data formatting | bytes 229376
